TPU v7x, 32 devices: a whole 2x2x4 slice. The times are simulated.
32 devices in a mesh: heads: 4 (over z), rows: 8 (over y, x, core).
Axes of the slice: x: 2, y: 2, z: 4, core: 2. Of those that a mesh axis runs over, the one named last changes fastest.
Arguments:
- tokens: bfloat16 [4, 2048, 1024], P(None, 'rows'), may hold values from -6 to 6
- cam_index: int32 [4, 2048], P(None, 'rows'), may hold values from 0 to 31
- patches: bfloat16 [4, 2048, 768], P(None, 'rows'), may hold values from -6 to 6
- patch_len: int32 [4], replicated, may hold values from 512 to 2048, as said below
- camera_table: bfloat16 [32, 2, 1024], replicated, may hold values from -3 to 3
- self_weights: bfloat16 [3, 1024, 1024], P(None, None, 'heads'), may hold values from -0.1875 to 0.1875
- self_output: bfloat16 [1024, 1024], P('heads'), may hold values from -4 to 4
- cross_gain: bfloat16 [1024], replicated, may hold values from 0.5 to 1.5
- cross_query: bfloat16 [1024, 1024], P(None, 'heads'), may hold values from -0.1875 to 0.1875
- cross_pair: bfloat16 [2, 1024, 1024], P(None, None, 'heads'), may hold values from -0.1875 to 0.1875
- cross_output: bfloat16 [1024, 1024], P('heads'), may hold values from -4 to 4
- patch_weights: bfloat16 [768, 1024], replicated, may hold values from -0.21875 to 0.21875
- hidden_gain: bfloat16 [1024], replicated, may hold values from 0.5 to 1.5
- widen_weights: bfloat16 [1024, 4096], P(None, 'heads'), may hold values from -0.1875 to 0.1875
- narrow_weights: bfloat16 [4096, 1024], P('heads'), may hold values from -0.09375 to 0.09375
- cotangent: bfloat16 [4, 2048, 1024], P(None, 'rows'), may hold values from -6 to 6
Outputs:
- tokens_out: bfloat16 [4, 2048, 1024], P(None, 'rows')
- input_grad: float32 [4, 2048, 1024], P(None, 'rows')
- patch_grad: float32 [4, 2048, 768], P(None, 'rows')
- grad_camera_table: float32 [32, 2, 1024], P(None, None, 'heads')
- grad_self_weights: float32 [3, 1024, 1024], P(None, None, 'heads')
- grad_self_output: float32 [1024, 1024], P('heads')
- grad_cross_gain: float32 [1024], P('heads')
- grad_cross_query: float32 [1024, 1024], P(None, 'heads')
- grad_cross_pair: float32 [2, 1024, 1024], P(None, None, 'heads')
- grad_cross_output: float32 [1024, 1024], P('heads')
- grad_patch_weights: float32 [768, 1024], P(None, 'heads')
- grad_hidden_gain: float32 [1024], P('heads')
- grad_widen_weights: float32 [1024, 4096], P(None, 'heads')
- grad_narrow_weights: float32 [4096, 1024], P('heads')
Inputs may be any that keep to these rules, and one draw needn't show every extreme that they name: `patch_len`: each entry is 2048 or a quarter of 2048; both values occur in every draw. Live patch tokens are the first ones of the object.
All inputs are finite; a program needn't handle non-finite values.
Results may differ from a plain program's by a relative error of at most 0.028.
The roundings to bfloat16 on the way count: a program that leaves them out, or rounds other values in their place, can miss the bound.
Values may be sent and summed in bfloat16 or wider, within the bound.
No kernel may reach another device: no remote copies, remote signals or barrier semaphores. Data moves between devices by JAX's collectives and lax.ppermute only.
A program may use at most 448 MiB of HBM per device.

v0:
```python
from functools import reduce
import jax
import jax.numpy as jnp
from jax import lax
from jax.sharding import PartitionSpec as P

HEAD_DIM = 64
EPSILON = 1e-05


def layer_norm(inputs):
    centred = inputs - jnp.mean(inputs, axis=-1, keepdims=True)
    return centred * lax.rsqrt(jnp.mean(centred * centred, axis=-1, keepdims=True) + EPSILON)


def modulated(inputs, shift_scale):
    return layer_norm(inputs) * (1.0 + shift_scale[:, 0]) + shift_scale[:, 1]


def gained(inputs, gain_row):
    return layer_norm(inputs) * gain_row


def gelu_tanh(pre_act):
    return jax.nn.gelu(pre_act, approximate=True)


def by_heads(matrix):
    return matrix.reshape(matrix.shape[0], -1, HEAD_DIM)


def scaled_scores(queries, key_rows):
    return jnp.einsum(
        "qhe,khe->hqk", queries, key_rows, preferred_element_type=jnp.float32
    ) * HEAD_DIM ** (-0.5)


def attend_forward(queries, key_rows, value_rows, mask_add):
    scores = scaled_scores(queries, key_rows) + mask_add
    row_peak = jnp.max(scores, axis=-1, keepdims=True)
    raised = jnp.exp(scores - row_peak)
    row_total = jnp.sum(raised, axis=-1, keepdims=True)
    attn_probs = (raised / row_total).astype(jnp.bfloat16)
    mixed_out = jnp.einsum(
        "hqk,khe->qhe", attn_probs, value_rows, preferred_element_type=jnp.float32
    )
    return (mixed_out.reshape(mixed_out.shape[0], -1).astype(jnp.bfloat16), row_peak, row_total)


def attend_queries_back(queries, key_rows, value_rows, mask_add, row_peak, row_total, grad_mixed):
    score_scale = HEAD_DIM ** (-0.5)
    scores = scaled_scores(queries, key_rows) + mask_add
    attn_probs = jnp.exp(scores - row_peak) / row_total
    grad_probs = jnp.einsum(
        "qhe,khe->hqk", grad_mixed, value_rows, preferred_element_type=jnp.float32
    )
    spread = jnp.sum(attn_probs * grad_probs, axis=-1, keepdims=True)
    grad_scores = (attn_probs * (grad_probs - spread)).astype(jnp.bfloat16)
    grad_queries = (
        jnp.einsum("hqk,khe->qhe", grad_scores, key_rows, preferred_element_type=jnp.float32)
        * score_scale
    )
    return (grad_queries, spread)


def attend_keys_back(
    all_queries, key_rows, value_rows, mask_add, all_peak, all_total, all_spread, all_grad
):
    score_scale = HEAD_DIM ** (-0.5)
    scores = scaled_scores(all_queries, key_rows) + mask_add
    attn_probs = jnp.exp(scores - all_peak) / all_total
    grad_probs = jnp.einsum(
        "qhe,khe->hqk", all_grad, value_rows, preferred_element_type=jnp.float32
    )
    grad_scores = (attn_probs * (grad_probs - all_spread)).astype(jnp.bfloat16)
    grad_keys = (
        jnp.einsum("hqk,qhe->khe", grad_scores, all_queries, preferred_element_type=jnp.float32)
        * score_scale
    )
    grad_values = jnp.einsum(
        "hqk,qhe->khe",
        attn_probs.astype(jnp.bfloat16),
        all_grad,
        preferred_element_type=jnp.float32,
    )
    return (grad_keys, grad_values)


def owner_key_grads(
    queries, grad_mixed, row_peak, row_total, spread, own_keys, own_values, own_mask
):
    gathered_queries, gathered_grads = (
        lax.all_gather(queries, "rows", axis=0, tiled=True),
        lax.all_gather(grad_mixed, "rows", axis=0, tiled=True),
    )
    gathered_peak, gathered_total, gathered_spread = (
        lax.all_gather(row_peak[:, :, 0].T, "rows", axis=0, tiled=True),
        lax.all_gather(row_total[:, :, 0].T, "rows", axis=0, tiled=True),
        lax.all_gather(spread[:, :, 0].T, "rows", axis=0, tiled=True),
    )
    grad_keys, grad_values = attend_keys_back(
        by_heads(gathered_queries),
        by_heads(own_keys),
        by_heads(own_values),
        own_mask,
        gathered_peak.T[:, :, None],
        gathered_total.T[:, :, None],
        gathered_spread.T[:, :, None],
        by_heads(gathered_grads),
    )
    return (grad_keys.reshape(own_keys.shape[0], -1), grad_values.reshape(own_keys.shape[0], -1))


def add_trees(former, latter):
    return jax.tree.map(jnp.add, former, latter)


def per_device(
    tokens,
    cam_index,
    patches,
    patch_len,
    camera_table,
    self_weights,
    self_output,
    cross_gain,
    cross_query,
    cross_pair,
    cross_output,
    patch_weights,
    hidden_gain,
    widen_weights,
    narrow_weights,
    cotangent,
):
    batches = tokens.shape[0]
    row_count = tokens.shape[1]
    model_width = tokens.shape[2]
    local_cols = self_weights.shape[2]
    code_count = camera_table.shape[0]
    patch_rows = patches.shape[1]
    row_rank = lax.axis_index("rows")
    head_rank = lax.axis_index("heads")
    all_patches = patch_rows * lax.axis_size("rows")
    table_flat = camera_table.reshape(code_count, -1).astype(jnp.float32)
    patch_index = jnp.arange(all_patches)
    own_index = row_rank * patch_rows + jnp.arange(patch_rows)
    cross_gain_f = cross_gain.astype(jnp.float32)
    hidden_gain_f = hidden_gain.astype(jnp.float32)
    outputs = []
    input_grads = []
    patch_grads = []
    contributions = []
    for microbatch in range(batches):
        inputs = tokens[microbatch].astype(jnp.float32)
        onehot = (cam_index[microbatch][:, None] == jnp.arange(code_count)[None, :]).astype(
            jnp.float32
        )
        shift_scale = jnp.dot(onehot, table_flat, precision=lax.Precision.HIGHEST).reshape(
            row_count, 2, model_width
        )
        normed_one, norm_one_back = jax.vjp(modulated, inputs, shift_scale)
        normed_one_low = normed_one.astype(jnp.bfloat16)
        projected = jnp.einsum(
            "rd,tdc->trc", normed_one_low, self_weights, preferred_element_type=jnp.float32
        ).astype(jnp.bfloat16)
        queries = projected[0]
        all_keys, all_values = (
            lax.all_gather(projected[1], "rows", axis=0, tiled=True),
            lax.all_gather(projected[2], "rows", axis=0, tiled=True),
        )
        self_mixed, self_peak, self_total = attend_forward(
            by_heads(queries), by_heads(all_keys), by_heads(all_values), 0.0
        )
        attn_sum = lax.psum(
            jnp.dot(self_mixed, self_output, preferred_element_type=jnp.float32), "heads"
        )
        after_self = inputs + attn_sum
        normed_two, norm_two_back = jax.vjp(gained, after_self, cross_gain_f)
        normed_two_low = normed_two.astype(jnp.bfloat16)
        cross_queries = jnp.dot(
            normed_two_low, cross_query, preferred_element_type=jnp.float32
        ).astype(jnp.bfloat16)
        patch_mid = jnp.dot(
            patches[microbatch], patch_weights, preferred_element_type=jnp.float32
        ).astype(jnp.bfloat16)
        patch_pair = jnp.einsum(
            "pd,tdc->tpc", patch_mid, cross_pair, preferred_element_type=jnp.float32
        ).astype(jnp.bfloat16)
        own_keys = patch_pair[0]
        own_values = patch_pair[1]
        cross_keys_all, cross_values_all = (
            lax.all_gather(own_keys, "rows", axis=0, tiled=True),
            lax.all_gather(own_values, "rows", axis=0, tiled=True),
        )
        mask_add = jnp.where(patch_index < patch_len[microbatch], 0.0, -1e30).astype(jnp.float32)
        cross_mixed, cross_peak, cross_total = attend_forward(
            by_heads(cross_queries), by_heads(cross_keys_all), by_heads(cross_values_all), mask_add
        )
        cross_sum = lax.psum(
            jnp.dot(cross_mixed, cross_output, preferred_element_type=jnp.float32).astype(
                jnp.bfloat16
            ),
            "heads",
        ).astype(jnp.float32)
        after_cross = after_self + cross_sum
        normed_three, norm_three_back = jax.vjp(gained, after_cross, hidden_gain_f)
        normed_three_low = normed_three.astype(jnp.bfloat16)
        pre_act = jnp.dot(normed_three_low, widen_weights, preferred_element_type=jnp.float32)
        activated, act_back = jax.vjp(gelu_tanh, pre_act)
        activated_low = activated.astype(jnp.bfloat16)
        hidden_sum = lax.psum(
            jnp.dot(activated_low, narrow_weights, preferred_element_type=jnp.float32).astype(
                jnp.bfloat16
            ),
            "heads",
        ).astype(jnp.float32)
        outputs.append((after_cross + hidden_sum).astype(jnp.bfloat16))
        grad_low = cotangent[microbatch]
        grad_top = grad_low.astype(jnp.float32)
        narrow_term = jnp.einsum(
            "rf,rd->fd", activated_low, grad_low, preferred_element_type=jnp.float32
        )
        grad_act = jnp.einsum(
            "rd,fd->rf", grad_low, narrow_weights, preferred_element_type=jnp.float32
        )
        grad_pre = act_back(grad_act)[0].astype(jnp.bfloat16)
        widen_term = jnp.einsum(
            "rd,rf->df", normed_three_low, grad_pre, preferred_element_type=jnp.float32
        )
        grad_normed_three = lax.psum(
            jnp.einsum(
                "rf,df->rd", grad_pre, widen_weights, preferred_element_type=jnp.float32
            ).astype(jnp.bfloat16),
            "heads",
        ).astype(jnp.float32)
        grad_mid, hidden_gain_term = norm_three_back(grad_normed_three)
        grad_cross = grad_top + grad_mid
        grad_cross_low = grad_cross.astype(jnp.bfloat16)
        cross_output_term = jnp.einsum(
            "rc,rd->cd", cross_mixed, grad_cross_low, preferred_element_type=jnp.float32
        )
        grad_cross_mixed = jnp.einsum(
            "rd,cd->rc", grad_cross_low, cross_output, preferred_element_type=jnp.float32
        ).astype(jnp.bfloat16)
        grad_cq, cross_spread = attend_queries_back(
            by_heads(cross_queries),
            by_heads(cross_keys_all),
            by_heads(cross_values_all),
            mask_add,
            cross_peak,
            cross_total,
            by_heads(grad_cross_mixed),
        )
        own_mask = jnp.where(own_index < patch_len[microbatch], 0.0, -1e30).astype(jnp.float32)
        grad_ck, grad_cv = owner_key_grads(
            cross_queries,
            grad_cross_mixed,
            cross_peak,
            cross_total,
            cross_spread,
            own_keys,
            own_values,
            own_mask,
        )
        grad_pair_low = jnp.stack([grad_ck, grad_cv]).astype(jnp.bfloat16)
        pair_term = jnp.einsum(
            "pd,tpc->tdc", patch_mid, grad_pair_low, preferred_element_type=jnp.float32
        )
        grad_cq_low = grad_cq.reshape(row_count, -1).astype(jnp.bfloat16)
        query_term = jnp.einsum(
            "rd,rc->dc", normed_two_low, grad_cq_low, preferred_element_type=jnp.float32
        )
        grad_normed_two, grad_patch_mid = (
            lax.psum(
                jnp.einsum(
                    "rc,dc->rd", grad_cq_low, cross_query, preferred_element_type=jnp.float32
                ).astype(jnp.bfloat16),
                "heads",
            ).astype(jnp.float32),
            lax.psum(
                jnp.einsum(
                    "tpc,tdc->pd", grad_pair_low, cross_pair, preferred_element_type=jnp.float32
                ).astype(jnp.bfloat16),
                "heads",
            ).astype(jnp.float32),
        )
        grad_mid_low = grad_patch_mid.astype(jnp.bfloat16)
        own_columns = lax.dynamic_slice_in_dim(grad_mid_low, head_rank * local_cols, local_cols, 1)
        patch_term = jnp.einsum(
            "pe,pc->ec", patches[microbatch], own_columns, preferred_element_type=jnp.float32
        )
        patch_grads.append(
            jnp.einsum("pd,ed->pe", grad_mid_low, patch_weights, preferred_element_type=jnp.float32)
        )
        grad_after_self, cross_gain_term = norm_two_back(grad_normed_two)
        grad_self = grad_cross + grad_after_self
        grad_self_low = grad_self.astype(jnp.bfloat16)
        self_output_term = jnp.einsum(
            "rc,rd->cd", self_mixed, grad_self_low, preferred_element_type=jnp.float32
        )
        grad_self_mixed = jnp.einsum(
            "rd,cd->rc", grad_self_low, self_output, preferred_element_type=jnp.float32
        ).astype(jnp.bfloat16)
        grad_q, self_spread = attend_queries_back(
            by_heads(queries),
            by_heads(all_keys),
            by_heads(all_values),
            0.0,
            self_peak,
            self_total,
            by_heads(grad_self_mixed),
        )
        grad_k, grad_v = owner_key_grads(
            queries,
            grad_self_mixed,
            self_peak,
            self_total,
            self_spread,
            projected[1],
            projected[2],
            0.0,
        )
        grad_proj = jnp.stack([grad_q.reshape(row_count, -1), grad_k, grad_v]).astype(jnp.bfloat16)
        self_term = jnp.einsum(
            "rd,trc->tdc", normed_one_low, grad_proj, preferred_element_type=jnp.float32
        )
        grad_normed_one = lax.psum(
            jnp.einsum(
                "trc,tdc->rd", grad_proj, self_weights, preferred_element_type=jnp.float32
            ).astype(jnp.bfloat16),
            "heads",
        ).astype(jnp.float32)
        grad_inputs, grad_shift_scale = norm_one_back(grad_normed_one)
        table_term = jnp.dot(
            onehot.T, grad_shift_scale.reshape(row_count, -1), precision=lax.Precision.HIGHEST
        )
        input_grads.append(grad_self + grad_inputs)
        contributions.append(
            (
                table_term,
                self_term,
                self_output_term,
                cross_gain_term,
                query_term,
                pair_term,
                cross_output_term,
                patch_term,
                hidden_gain_term,
                widen_term,
                narrow_term,
            )
        )
    summed = reduce(add_trees, contributions)
    table_part = lax.dynamic_slice_in_dim(
        summed[0].reshape(code_count, 2, model_width), head_rank * local_cols, local_cols, 2
    )
    cross_gain_part = lax.dynamic_slice_in_dim(summed[3], head_rank * local_cols, local_cols, 0)
    hidden_gain_part = lax.dynamic_slice_in_dim(summed[8], head_rank * local_cols, local_cols, 0)
    totals = (
        lax.psum(table_part.astype(jnp.bfloat16), "rows").astype(jnp.float32),
        lax.psum(summed[1].astype(jnp.bfloat16), "rows").astype(jnp.float32),
        lax.psum(summed[2].astype(jnp.bfloat16), "rows").astype(jnp.float32),
        lax.psum(cross_gain_part.astype(jnp.bfloat16), "rows").astype(jnp.float32),
        lax.psum(summed[4].astype(jnp.bfloat16), "rows").astype(jnp.float32),
        lax.psum(summed[5].astype(jnp.bfloat16), "rows").astype(jnp.float32),
        lax.psum(summed[6].astype(jnp.bfloat16), "rows").astype(jnp.float32),
        lax.psum(summed[7].astype(jnp.bfloat16), "rows").astype(jnp.float32),
        lax.psum(hidden_gain_part.astype(jnp.bfloat16), "rows").astype(jnp.float32),
        lax.psum(summed[9].astype(jnp.bfloat16), "rows").astype(jnp.float32),
        lax.psum(summed[10].astype(jnp.bfloat16), "rows").astype(jnp.float32),
    )
    return (jnp.stack(outputs), jnp.stack(input_grads), jnp.stack(patch_grads)) + tuple(totals)


def solution(mesh):
    in_specs = (
        P(None, "rows", None),
        P(None, "rows"),
        P(None, "rows", None),
        P(),
        P(),
        P(None, None, "heads"),
        P("heads", None),
        P(),
        P(None, "heads"),
        P(None, None, "heads"),
        P("heads", None),
        P(),
        P(),
        P(None, "heads"),
        P("heads", None),
        P(None, "rows", None),
    )
    out_specs = (
        P(None, "rows", None),
        P(None, "rows", None),
        P(None, "rows", None),
        P(None, None, "heads"),
        P(None, None, "heads"),
        P("heads", None),
        P("heads"),
        P(None, "heads"),
        P(None, None, "heads"),
        P("heads", None),
        P(None, "heads"),
        P("heads"),
        P(None, "heads"),
        P("heads", None),
    )
    return jax.shard_map(
        per_device, mesh=mesh, in_specs=in_specs, out_specs=out_specs, check_vma=False
    )
```

profile of v0, /device:TPU:0, one launch (start us, length us, event | category | flops | bytes accessed | tf_op | source)
XLA Modules:
  0.0 1912.5 jit_solution(12267981073876656317)
XLA Ops:
  36.8 9.2 all-gather.87.cloned.1.call-done
  53.8 17.8 all-gather.85.cloned.1.call-done
  78.5 19.1 all-gather.103.cloned.1.call-done
  105.1 17.8 all-gather.101.cloned.1.call-done
  128.6 20.3 %all-gather.95.cloned.1.call-done = bf16[1,2048,256]{1,2,0:T(8,128)(2,1)} async-done(((bf16[1,256,256]{1,2,0:T(8,128)(2,1)}), bf16[1,2048,256]{1,2,0:T(8,128)(2,1)}) %all-gather.95.cloned.1.call-update) | async-done | bytes 1048592 | tf_op jit(solution)/shard_map/all_gather | solution.py:169
  156.3 17.9 all-gather.93.cloned.1.call-done
  179.8 19.8 %all-gather.79.cloned.1.call-done = bf16[1,2048,256]{1,2,0:T(8,128)(2,1)} async-done(((bf16[1,256,256]{1,2,0:T(8,128)(2,1)}), bf16[1,2048,256]{1,2,0:T(8,128)(2,1)}) %all-gather.79.cloned.1.call-update) | async-done | bytes 1048592 | tf_op jit(solution)/shard_map/all_gather | solution.py:169
  210.0 15.2 all-gather.77.cloned.1.call-done
  262.0 9.0 all_gather.196
  271.0 8.1 all_gather.195
  279.1 9.0 all_gather.191
  288.1 8.1 all_gather.190
  296.2 9.0 all_gather.186
  305.3 8.1 all_gather.185
  331.8 9.1 all_gather.201
  341.0 8.1 all_gather.200
  349.1 112.7 %all-reduce.22.cloned.1.call-done = (f32[256,1024]{1,0:T(8,128)}, f32[256,1024]{1,0:T(8,128)}, f32[256,1024]{1,0:T(8,128)}, f32[256,1024]{1,0:T(8,128)}) async-done(((f32[256,1024]{1,0:T(8,128)}, f32[256,1024]{1,0:T(8,128)}, f32[256,1024]{1,0:T(8,128)}, f32[256,1024]{1,0:T(8,128)}), (f32[256,1024]{1,0:T(8,128)}, f32[256,1024]{1,0:T(8,128)}, f32[256,1024]{1,0:T(8,128)}, ...) | async-done | bytes 4194320 | tf_op jit(solution)/shard_map/psum | solution.py:175
  469.0 17.5 all-gather.115.cloned.1.call-done
  494.1 17.8 all-gather.107.cloned.1.call-done
  516.7 10.0 all_gather.221
  526.7 9.1 all_gather.220
  547.5 15.5 all-gather.89.cloned.1.call-done
  568.9 19.6 %all-gather.83.cloned.1.call-done = bf16[1,2048,256]{1,2,0:T(8,128)(2,1)} async-done(((bf16[1,256,256]{1,2,0:T(8,128)(2,1)}), bf16[1,2048,256]{1,2,0:T(8,128)(2,1)}) %all-gather.83.cloned.1.call-update) | async-done | bytes 1048592 | tf_op jit(solution)/shard_map/all_gather | solution.py:193
  596.9 17.1 all-gather.81.cloned.1.call-done
  619.9 19.8 %all-gather.99.cloned.1.call-done = bf16[1,2048,256]{1,2,0:T(8,128)(2,1)} async-done(((bf16[1,256,256]{1,2,0:T(8,128)(2,1)}), bf16[1,2048,256]{1,2,0:T(8,128)(2,1)}) %all-gather.99.cloned.1.call-update) | async-done | bytes 1048592 | tf_op jit(solution)/shard_map/all_gather | solution.py:193
  647.5 10.0 all_gather.216
  657.5 9.1 all_gather.215
  666.6 10.4 all_gather.211
  685.1 9.1 all_gather.210
  694.2 9.9 all_gather.206
  704.2 9.1 all_gather.205
  729.4 12.9 all-gather.69.cloned.1.call-done
  748.4 19.4 %all-gather.65.cloned.1.call-done = bf16[2048,256]{0,1:T(8,128)(2,1)} async-done(((bf16[256,256]{0,1:T(8,128)(2,1)}), bf16[2048,256]{0,1:T(8,128)(2,1)}) %all-gather.65.cloned.1.call-update) | async-done | bytes 1048592 | tf_op jit(solution)/shard_map/all_gather | solution.py:93
  774.0 19.4 %all-gather.61.cloned.1.call-done = bf16[2048,256]{0,1:T(8,128)(2,1)} async-done(((bf16[256,256]{0,1:T(8,128)(2,1)}), bf16[2048,256]{0,1:T(8,128)(2,1)}) %all-gather.61.cloned.1.call-update) | async-done | bytes 1048592 | tf_op jit(solution)/shard_map/all_gather | solution.py:93
  799.6 85.7 %all-reduce.32.cloned.1.call-done = (bf16[256,1024]{1,0:T(8,128)(2,1)}, bf16[256,1024]{1,0:T(8,128)(2,1)}, bf16[256,1024]{1,0:T(8,128)(2,1)}, bf16[256,1024]{1,0:T(8,128)(2,1)}) async-done(((bf16[256,1024]{1,0:T(8,128)(2,1)}, bf16[256,1024]{1,0:T(8,128)(2,1)}, bf16[256,1024]{1,0:T(8,128)(2,1)}, bf16[256,1024]{1,0:T(8,128)(2,1)}), (bf16[256,1024]{1,0:T(8,128)(2,1)}, bf16[256,1024]{1,0:T(8,128)(2,1)}, ...) | async-done | bytes 2097168 | tf_op jit(solution)/shard_map/psum | solution.py:200
  940.0 68.7 %all-reduce.30.cloned.1.call-done = (bf16[256,1024]{1,0:T(8,128)(2,1)}, bf16[256,1024]{1,0:T(8,128)(2,1)}, bf16[256,1024]{1,0:T(8,128)(2,1)}, bf16[256,1024]{1,0:T(8,128)(2,1)}) async-done(((bf16[256,1024]{1,0:T(8,128)(2,1)}, bf16[256,1024]{1,0:T(8,128)(2,1)}, bf16[256,1024]{1,0:T(8,128)(2,1)}, bf16[256,1024]{1,0:T(8,128)(2,1)}), (bf16[256,1024]{1,0:T(8,128)(2,1)}, bf16[256,1024]{1,0:T(8,128)(2,1)}, ...) | async-done | bytes 2097168 | tf_op jit(solution)/shard_map/psum | solution.py:231
  1026.2 7.7 multiply_reduce_fusion.3
  1035.0 7.3 multiply_reduce_fusion.1
  1042.3 9.0 all_gather.223
  1051.4 9.0 all_gather.218
  1060.4 7.5 fusion.173
  1076.5 8.3 all_gather.213
  1084.8 7.7 fusion.171
  1093.7 9.0 all_gather.208
  1102.7 7.5 fusion.177
  1111.5 7.8 fusion.175
  1179.4 61.4 %all-reduce.28.cloned.1.call-done = (bf16[256,1024]{1,0:T(8,128)(2,1)}, bf16[256,1024]{1,0:T(8,128)(2,1)}, bf16[256,1024]{1,0:T(8,128)(2,1)}, bf16[256,1024]{1,0:T(8,128)(2,1)}) async-done(((bf16[256,1024]{1,0:T(8,128)(2,1)}, bf16[256,1024]{1,0:T(8,128)(2,1)}, bf16[256,1024]{1,0:T(8,128)(2,1)}, bf16[256,1024]{1,0:T(8,128)(2,1)}), (bf16[256,1024]{1,0:T(8,128)(2,1)}, bf16[256,1024]{1,0:T(8,128)(2,1)}, ...) | async-done | bytes 2097168 | tf_op jit(solution)/shard_map/psum | solution.py:275
  1264.1 8.1 multiply_reduce_fusion.2
  1272.3 10.3 multiply_reduce_fusion.4
  1283.0 8.1 multiply_reduce_fusion.6
  1293.0 9.3 fusion.176
  1302.4 8.1 fusion.174
  1326.3 8.5 fusion.178
  1335.6 10.7 all_gather.198
  1346.3 9.3 all_gather.193
  1355.6 10.2 all_gather.188
  1365.8 9.3 all_gather.203
  1380.7 7.1 fusion.165
  1391.1 7.1 fusion.164
  1406.8 7.1 fusion.163
  1427.6 7.1 fusion.166
  1471.0 204.0 %all-reduce.26.cloned.1.call-done = (bf16[256,1024]{1,0:T(8,128)(2,1)}, bf16[256,1024]{1,0:T(8,128)(2,1)}, bf16[256,1024]{1,0:T(8,128)(2,1)}, bf16[256,1024]{1,0...) async-done(((bf16[256,1024]{1,0:T(8,128)(2,1)}, ...) | async-done | bytes 6291472 | tf_op jit(solution)/shard_map/psum | solution.py:281
  1722.2 24.8 %all-reduce.9 = (bf16[32,2,256]{2,1,0:T(2,128)(2,1)S(1)}, bf16[256]{0:T(256)(128)(2,1)S(1)}, bf16[256]{0:T(256)(128)(2,1)S(1)}) all-reduce(bf16[32,2,256]{2,1,0:T(2,128)(2,1)S(1)} %dynamic-slice_convert_fusion, bf16[256]{0:T(256)(128)(2,1)S(1)} %dynamic_slice.40, ...), channel_id=1, replica_groups=mesh['heads'=4,'rows'=8] {'rows'}, use_global_device_ids=true, to_apply=%region_100.101 | all-reduce | flops 16896 | bytes 67584 | tf_op jit(solution)/shard_map/psum | solution.py:361
  1769.1 116.2 %all-reduce.24.cloned.1.call-done = (bf16[3,1024,256]{1,2,0:T(8,128)(2,1)}, bf16[2,1024,256]{1,2,0:T(8,128)(2,1)}, bf16[768,256]{0,1:T(8,128)(2,1)}, bf16[256,10...) async-done(((bf16[3,1024,256]{1,2,0:T(8,128)(2,1)}, ...) | async-done | bytes 8781840 | tf_op jit(solution)/shard_map/psum | solution.py:362
  (1070 shorter events, 577.8 us)
Async XLA Ops:
  7.2 880.9 %copy-start = (bf16[1024,1024]{1,0:T(8,128)(2,1)S(1)}, bf16[1024,1024]{1,0:T(8,128)(2,1)}, u32[]{:S(2)}) copy-start(bf16[1024,1024]{1,0:T(8,128)(2,1)} %param.29) | copy-start | bytes 6291460
  7.2 38.8 %all-gather.87.cloned.1.call-start = ((), (), s32[]{:S(2)}) async-start(), calls=%async_computation.17 | async-start | bytes 1179648 | tf_op jit(solution)/shard_map/all_gather | solution.py:169
  19.6 51.9 %all-gather.85.cloned.1.call-start = ((), (), s32[]{:S(2)}) async-start(), calls=%async_computation.16 | async-start | bytes 1179648 | tf_op jit(solution)/shard_map/all_gather | solution.py:170
  20.4 77.2 %all-gather.103.cloned.1.call-start = ((), (), s32[]{:S(2)}) async-start(), calls=%async_computation.25 | async-start | bytes 1179648 | tf_op jit(solution)/shard_map/all_gather | solution.py:169
  23.4 99.6 %all-gather.101.cloned.1.call-start = ((), (), s32[]{:S(2)}) async-start(), calls=%async_computation.24 | async-start | bytes 1179648 | tf_op jit(solution)/shard_map/all_gather | solution.py:170
  24.0 124.9 %all-gather.95.cloned.1.call-start = ((), (), s32[]{:S(2)}) async-start(), calls=%async_computation.21 | async-start | bytes 1179648 | tf_op jit(solution)/shard_map/all_gather | solution.py:169
  26.9 147.3 %all-gather.93.cloned.1.call-start = ((), (), s32[]{:S(2)}) async-start(), calls=%async_computation.20 | async-start | bytes 1179648 | tf_op jit(solution)/shard_map/all_gather | solution.py:170
  27.5 172.2 %all-gather.79.cloned.1.call-start = ((), (), s32[]{:S(2)}) async-start(), calls=%async_computation.13 | async-start | bytes 1179648 | tf_op jit(solution)/shard_map/all_gather | solution.py:169
  34.0 191.2 %all-gather.77.cloned.1.call-start = ((), (), s32[]{:S(2)}) async-start(), calls=%async_computation.12 | async-start | bytes 1179648 | tf_op jit(solution)/shard_map/all_gather | solution.py:170
  34.7 278.7 %all-gather.113.cloned.1.call-start = ((), (), s32[]{:S(2)}) async-start(), calls=%async_computation.30 | async-start | bytes 1179648 | tf_op jit(solution)/shard_map/all_gather | solution.py:93
  35.4 284.3 %all-gather.111.cloned.1.call-start = ((), (), s32[]{:S(2)}) async-start(), calls=%async_computation.29 | async-start | bytes 1179648 | tf_op jit(solution)/shard_map/all_gather | solution.py:93
  36.0 289.8 %all-gather.109.cloned.1.call-start = ((), (), s32[]{:S(2)}) async-start(), calls=%async_computation.28 | async-start | bytes 1179648 | tf_op jit(solution)/shard_map/all_gather | solution.py:93
  36.8 425.0 %all-reduce.22.cloned.1.call-start = ((), (), s32[]{:S(2)}) async-start(), calls=%async_computation.32 | async-start | bytes 8388608 | tf_op jit(solution)/shard_map/psum | solution.py:175
  53.8 225.4 %copy-start.262 = (f32[4,256]{1,0:T(4,128)}, f32[4,256]{1,0:T(4,128)S(1)}, u32[]{:S(2)}) copy-start(f32[4,256]{1,0:T(4,128)S(1)} %fusion.7) | copy-start | bytes 12292
  100.2 240.8 %copy-start.224 = (f32[4,256]{1,0:T(4,128)}, f32[4,256]{1,0:T(4,128)S(1)}, u32[]{:S(2)}) copy-start(f32[4,256]{1,0:T(4,128)S(1)} %get-tuple-element.215) | copy-start | bytes 12292
  105.1 226.7 %copy-start.260 = (f32[4,256]{1,0:T(4,128)}, f32[4,256]{1,0:T(4,128)S(1)}, u32[]{:S(2)}) copy-start(f32[4,256]{1,0:T(4,128)S(1)} %fusion.11) | copy-start | bytes 12292
  151.4 119.6 %copy-start.231 = (f32[4,256]{1,0:T(4,128)}, f32[4,256]{1,0:T(4,128)S(1)}, u32[]{:S(2)}) copy-start(f32[4,256]{1,0:T(4,128)S(1)} %get-tuple-element.213) | copy-start | bytes 12292
  156.3 105.7 %copy-start.266 = (f32[4,256]{1,0:T(4,128)}, f32[4,256]{1,0:T(4,128)S(1)}, u32[]{:S(2)}) copy-start(f32[4,256]{1,0:T(4,128)S(1)} %fusion.9) | copy-start | bytes 12292
  202.3 103.0 %copy-start.229 = (f32[4,256]{1,0:T(4,128)}, f32[4,256]{1,0:T(4,128)S(1)}, u32[]{:S(2)}) copy-start(f32[4,256]{1,0:T(4,128)S(1)} %get-tuple-element.217) | copy-start | bytes 12292
  207.4 88.9 %copy-start.264 = (f32[4,256]{1,0:T(4,128)}, f32[4,256]{1,0:T(4,128)S(1)}, u32[]{:S(2)}) copy-start(f32[4,256]{1,0:T(4,128)S(1)} %fusion.5) | copy-start | bytes 12292
  232.8 253.7 %all-gather.115.cloned.1.call-start = ((), (), s32[]{:S(2)}) async-start(), calls=%async_computation.31 | async-start | bytes 1179648 | tf_op jit(solution)/shard_map/all_gather | solution.py:93
  233.5 278.5 %all-gather.107.cloned.1.call-start = ((), (), s32[]{:S(2)}) async-start(), calls=%async_computation.27 | async-start | bytes 1179648 | tf_op jit(solution)/shard_map/all_gather | solution.py:193
  237.9 301.8 %all-gather.91.cloned.1.call-start = ((), (), s32[]{:S(2)}) async-start(), calls=%async_computation.19 | async-start | bytes 1179648 | tf_op jit(solution)/shard_map/all_gather | solution.py:193
  242.2 320.9 %all-gather.89.cloned.1.call-start = ((), (), s32[]{:S(2)}) async-start(), calls=%async_computation.18 | async-start | bytes 1179648 | tf_op jit(solution)/shard_map/all_gather | solution.py:194
  242.8 345.8 %all-gather.83.cloned.1.call-start = ((), (), s32[]{:S(2)}) async-start(), calls=%async_computation.15 | async-start | bytes 1179648 | tf_op jit(solution)/shard_map/all_gather | solution.py:193
  247.0 367.0 %all-gather.81.cloned.1.call-start = ((), (), s32[]{:S(2)}) async-start(), calls=%async_computation.14 | async-start | bytes 1179648 | tf_op jit(solution)/shard_map/all_gather | solution.py:194
  247.6 392.0 %all-gather.99.cloned.1.call-start = ((), (), s32[]{:S(2)}) async-start(), calls=%async_computation.23 | async-start | bytes 1179648 | tf_op jit(solution)/shard_map/all_gather | solution.py:193
  251.3 427.8 %all-gather.105.cloned.1.call-start = ((), (), s32[]{:S(2)}) async-start(), calls=%async_computation.26 | async-start | bytes 1179648 | tf_op jit(solution)/shard_map/all_gather | solution.py:194
  251.9 463.5 %all-gather.97.cloned.1.call-start = ((), (), s32[]{:S(2)}) async-start(), calls=%async_computation.22 | async-start | bytes 1179648 | tf_op jit(solution)/shard_map/all_gather | solution.py:194
  252.7 470.6 %all-gather.73.cloned.1.call-start = ((), (), s32[]{:S(2)}) async-start(), calls=%async_computation.10 | async-start | bytes 1179648 | tf_op jit(solution)/shard_map/all_gather | solution.py:93
  257.7 284.6 %copy-start.215 = (f32[2048]{0:T(1024)}, f32[2048]{0:T(1024)S(1)}, u32[]{:S(2)}) copy-start(f32[2048]{0:T(1024)S(1)} %fusion.404) | copy-start | bytes 24580
  261.4 276.2 %copy-start.155 = (f32[1024]{0:T(1024)}, f32[1024]{0:T(1024)S(1)}, u32[]{:S(2)}) copy-start(f32[1024]{0:T(1024)S(1)} %convert_element_type.678) | copy-start | bytes 12292
  331.8 154.6 %copy-start.188 = (bf16[1,256,256]{1,2,0:T(8,128)(2,1)S(1)}, bf16[1,256,256]{1,2,0:T(8,128)(2,1)}, u32[]{:S(2)}) copy-start(bf16[1,256,256]{1,2,0:T(8,128)(2,1)} %get-tuple-element.177) | copy-start | bytes 393220
  466.4 431.6 %copy-start.7 = (f32[256,1024]{1,0:T(8,128)}, f32[256,1024]{1,0:T(8,128)S(1)}, u32[]{:S(2)}) copy-start(f32[256,1024]{1,0:T(8,128)S(1)} %get-tuple-element.167) | copy-start | bytes 3145732
  468.9 273.4 %all-gather.69.cloned.1.call-start = ((), (), s32[]{:S(2)}) async-start(), calls=%async_computation.8 | async-start | bytes 1179648 | tf_op jit(solution)/shard_map/all_gather | solution.py:93
  494.1 273.7 %all-gather.65.cloned.1.call-start = ((), (), s32[]{:S(2)}) async-start(), calls=%async_computation.6 | async-start | bytes 1179648 | tf_op jit(solution)/shard_map/all_gather | solution.py:93
  539.4 254.0 %all-gather.61.cloned.1.call-start = ((), (), s32[]{:S(2)}) async-start(), calls=%async_computation.4 | async-start | bytes 1179648 | tf_op jit(solution)/shard_map/all_gather | solution.py:93
  568.9 108.0 %copy-start.208 = (bf16[4,64,256]{2,1,0:T(8,128)(2,1)}, bf16[4,64,256]{2,1,0:T(8,128)(2,1)S(1)}, u32[]{:S(2)}) copy-start(bf16[4,64,256]{2,1,0:T(8,128)(2,1)S(1)} %fusion.188) | copy-start | bytes 393220
  685.1 200.2 %all-reduce.32.cloned.1.call-start = ((), (), s32[]{:S(2)}) async-start(), calls=%async_computation.37 | async-start | bytes 4194304 | tf_op jit(solution)/shard_map/psum | solution.py:200
  723.2 285.5 %all-reduce.30.cloned.1.call-start = ((), (), s32[]{:S(2)}) async-start(), calls=%async_computation.36 | async-start | bytes 4194304 | tf_op jit(solution)/shard_map/psum | solution.py:231
  793.4 94.7 %copy-start.142 = (f32[1024]{0:T(1024)S(1)}, f32[1024]{0:T(1024)}, u32[]{:S(2)}) copy-start(f32[1024]{0:T(1024)} %convert_element_type.687) | copy-start | bytes 12292
  921.5 200.4 %all-gather.75.cloned.1.call-start = ((), (), s32[]{:S(2)}) async-start(), calls=%async_computation.11 | async-start | bytes 1179648 | tf_op jit(solution)/shard_map/all_gather | solution.py:94
  1035.0 97.8 %all-gather.71.cloned.1.call-start = ((), (), s32[]{:S(2)}) async-start(), calls=%async_computation.9 | async-start | bytes 1179648 | tf_op jit(solution)/shard_map/all_gather | solution.py:94
  1076.4 67.8 %all-gather.67.cloned.1.call-start = ((), (), s32[]{:S(2)}) async-start(), calls=%async_computation.7 | async-start | bytes 1179648 | tf_op jit(solution)/shard_map/all_gather | solution.py:94
  1093.7 62.6 %all-gather.63.cloned.1.call-start = ((), (), s32[]{:S(2)}) async-start(), calls=%async_computation.5 | async-start | bytes 1179648 | tf_op jit(solution)/shard_map/all_gather | solution.py:94
  1111.5 129.3 %all-reduce.28.cloned.1.call-start = ((), (), s32[]{:S(2)}) async-start(), calls=%async_computation.35 | async-start | bytes 4194304 | tf_op jit(solution)/shard_map/psum | solution.py:275
  1121.9 253.6 %all-gather.57.cloned.1.call-start = ((), (), s32[]{:S(2)}) async-start(), calls=%async_computation.2 | async-start | bytes 1179648 | tf_op jit(solution)/shard_map/all_gather | solution.py:94
  1163.9 79.6 %copy-start.11 = (f32[256,1024]{1,0:T(8,128)S(1)}, f32[256,1024]{1,0:T(8,128)}, u32[]{:S(2)}) copy-start(f32[256,1024]{1,0:T(8,128)} %get-tuple-element.163) | copy-start | bytes 3145732
  1164.0 79.6 %copy-start.220 = (f32[256]{0:T(256)S(1)}, f32[256]{0:T(256)}, u32[]{:S(2)}) copy-start(f32[256]{0:T(256)} %copy-done.219) | copy-start | bytes 3076
  1164.0 79.6 %copy-start.222 = (f32[256]{0:T(256)S(1)}, f32[256]{0:T(256)}, u32[]{:S(2)}) copy-start(f32[256]{0:T(256)} %copy-done.221) | copy-start | bytes 3076
  1258.2 132.9 %all-gather.55.cloned.1.call-start = ((), (), s32[]{:S(2)}) async-start(), calls=%async_computation.1 | async-start | bytes 1179648 | tf_op jit(solution)/shard_map/all_gather | solution.py:94
  1272.2 134.5 %all-gather.53.cloned.1.call-start = ((), (), s32[]{:S(2)}) async-start(), calls=%async_computation | async-start | bytes 1179648 | tf_op jit(solution)/shard_map/all_gather | solution.py:94
  1291.0 131.4 %all-gather.59.cloned.1.call-start = ((), (), s32[]{:S(2)}) async-start(), calls=%async_computation.3 | async-start | bytes 1179648 | tf_op jit(solution)/shard_map/all_gather | solution.py:94
  1375.2 299.8 %all-reduce.26.cloned.1.call-start = ((), (), s32[]{:S(2)}) async-start(), calls=%async_computation.34 | async-start | bytes 12582912 | tf_op jit(solution)/shard_map/psum | solution.py:281
  1449.2 436.1 %all-reduce.24.cloned.1.call-start = ((), (), s32[]{:S(2)}) async-start(), calls=%async_computation.33 | async-start | bytes 17563648 | tf_op jit(solution)/shard_map/psum | solution.py:362
  1469.0 212.1 %copy-start.4 = (bf16[4,256,1024]{2,1,0:T(8,128)(2,1)S(1)}, bf16[4,256,1024]{2,1,0:T(8,128)(2,1)}, u32[]{:S(2)}) copy-start(bf16[4,256,1024]{2,1,0:T(8,128)(2,1)} %param.16) | copy-start | bytes 6291460
  1469.0 212.1 %copy-start.246 = (f32[256]{0:T(256)S(1)}, f32[256]{0:T(256)}, u32[]{:S(2)}) copy-start(f32[256]{0:T(256)} %copy-done.245) | copy-start | bytes 3076
  1469.0 212.1 %copy-start.248 = (f32[256]{0:T(256)S(1)}, f32[256]{0:T(256)}, u32[]{:S(2)}) copy-start(f32[256]{0:T(256)} %copy-done.247) | copy-start | bytes 3076
  1469.1 212.1 %copy-start.250 = (f32[256]{0:T(256)S(1)}, f32[256]{0:T(256)}, u32[]{:S(2)}) copy-start(f32[256]{0:T(256)} %copy-done.249) | copy-start | bytes 3076
  1469.1 212.1 %copy-start.252 = (f32[256]{0:T(256)S(1)}, f32[256]{0:T(256)}, u32[]{:S(2)}) copy-start(f32[256]{0:T(256)} %copy-done.251) | copy-start | bytes 3076
  1471.0 217.4 %copy-start.305 = (f32[256]{0:T(256)S(1)}, f32[256]{0:T(256)}, u32[]{:S(2)}) copy-start(f32[256]{0:T(256)} %copy-done.304) | copy-start | bytes 3076
  1471.0 217.4 %copy-start.303 = (f32[256]{0:T(256)S(1)}, f32[256]{0:T(256)}, u32[]{:S(2)}) copy-start(f32[256]{0:T(256)} %copy-done.302) | copy-start | bytes 3076
  1471.0 217.5 %copy-start.285 = (f32[256]{0:T(256)S(1)}, f32[256]{0:T(256)}, u32[]{:S(2)}) copy-start(f32[256]{0:T(256)} %copy-done.284) | copy-start | bytes 3076
  1471.0 217.5 %copy-start.287 = (f32[256]{0:T(256)S(1)}, f32[256]{0:T(256)}, u32[]{:S(2)}) copy-start(f32[256]{0:T(256)} %copy-done.286) | copy-start | bytes 3076
  (309 other events, 4190.8 us)
Sparse Core Ops, SparseCore 0:
  19.8 26.2 all-gather.86
  47.9 23.5 all-gather.84
  74.0 23.5 all-gather.102
  99.3 23.5 all-gather.100
  125.2 23.5 all-gather.94
  150.6 23.5 all-gather.92
  176.1 23.5 all-gather.78
  201.5 23.5 all-gather.76
  227.6 23.5 all-gather.112
  252.9 23.6 all-gather.110
  278.5 23.6 all-gather.108
  305.7 156.0 all-reduce.21
  463.8 22.6 all-gather.114
  488.4 23.5 all-gather.106
  513.9 23.6 all-gather.90
  539.4 23.5 all-gather.88
  564.9 23.5 all-gather.82
  590.4 23.5 all-gather.80
  616.0 23.5 all-gather.98
  641.5 23.7 all-gather.104
  667.3 23.5 all-gather.96
  693.0 23.6 all-gather.72
  718.7 23.5 all-gather.68
  744.2 23.5 all-gather.64
  769.8 23.5 all-gather.60
  797.2 88.0 all-reduce.31
  921.6 86.9 all-reduce.29
  1035.1 22.6 all-gather.74
  1076.5 21.6 all-gather.70
  1100.1 23.6 all-gather.66
  1126.3 23.5 all-gather.62
  1152.7 87.9 all-reduce.27
  1258.3 22.4 all-gather.56
  1282.7 23.5 all-gather.54
  1308.8 23.6 all-gather.52
  1375.3 22.0 all-gather.58
  1449.3 225.6 all-reduce.25
  1754.9 130.3 all-reduce.23
where the time goes:
time: 1920 us; the launch traced here: 1910 us
  waiting for transfers between devices  953 us (50%)
  matrix products  489 us (25%)
  blocking collectives  245 us (13%)
  other arithmetic  120 us (6%)
  local copies, waits for them, and re-layouts  84.7 us (4%)
    psum x1, waiting for transfers between devices, per_device(): lax.psum(jnp.einsum('tpc,tdc->pd', grad_pair_low, cross_pair, preferred_e...  204 us
    psum x1, waiting for transfers between devices, per_device(): lax.psum(summed[1].astype(jnp.bfloat16), 'rows').astype(jnp.float32)  116 us
    psum x1, waiting for transfers between devices, per_device(): lax.psum(jnp.dot(self_mixed, self_output, preferred_element_type=jnp.floa...  113 us
    psum x1, waiting for transfers between devices, per_device(): lax.psum(jnp.dot(cross_mixed, cross_output, preferred_element_type=jnp.fl...  85.7 us
    all_gather x8, blocking collectives, owner_key_grads(): lax.all_gather(row_total[:, :, 0].T, 'rows', axis=0, tiled=True)  76.4 us
    all_gather x8, blocking collectives, owner_key_grads(): lax.all_gather(spread[:, :, 0].T, 'rows', axis=0, tiled=True)  74.8 us
    dot_general x16, matrix products, scaled_scores(): jnp.einsum('qhe,khe->hqk', queries, key_rows, preferred_element_type=jnp....  70.2 us
    all_gather x8, waiting for transfers between devices, owner_key_grads(): lax.all_gather(queries, 'rows', axis=0, tiled=True)  69.2 us
  transfers between devices with their start and end apart: 38, of which 23 were waited for; matrix products, arithmetic and copies ran while one was open for 24% of the time, Pallas kernels for 0%

commit v1 on v0

--- a/solution.py
+++ b/solution.py
@@ -94,7 +94,10 @@
         lax.all_gather(grad_mixed, "rows", axis=0, tiled=True),
     )
     gathered_peak, gathered_total, gathered_spread = (
-        lax.all_gather(row_peak[:, :, 0].T, "rows", axis=0, tiled=True),
+        jnp.concatenate(
+            lax.all_to_all(jnp.stack([row_peak[:, :, 0].T] * lax.axis_size("rows")), "rows", 0, 0),
+            axis=0,
+        ),
         lax.all_gather(row_total[:, :, 0].T, "rows", axis=0, tiled=True),
         lax.all_gather(spread[:, :, 0].T, "rows", axis=0, tiled=True),
     )

time: 1920 us -> 1920 us (level)
  blocking collectives: 245 us -> 172 us
  starting transfers between devices: 2.1 us -> 33.5 us
  waiting for transfers between devices: 953 us -> 982 us
    all_gather x8 -> x0, blocking collectives: 68.9 us -> none  [owner_key_grads(): lax.all_gather(row_peak[:, :, 0].T, 'rows', axis=0, tiled=True)]
    all_gather x4, waiting for transfers between devices: 32.6 us -> 65.5 us  [per_device(): lax.all_gather(own_values, 'rows', axis=0, tiled=True)]
    all_to_all x0 -> x8, starting transfers between devices: none -> 31.4 us  [owner_key_grads(): lax.all_to_all(jnp.stack([row_peak[:, :, 0].T] * lax.axis_size('rows')),...]
    all_gather x8, waiting for transfers between devices: 69.2 us -> 44.9 us  [owner_key_grads(): lax.all_gather(queries, 'rows', axis=0, tiled=True)]
    unnamed x673 -> x663, local copies, waits for them, and re-layouts: 42.7 us -> 43.2 us
  transfers between devices with their start and end apart: 38 -> 46, of which waited for: 23 -> 25; matrix products, arithmetic and copies ran while one was open for 24% -> 25% of each run, Pallas kernels for 0% -> 0%
where the time goes in v1:
time: 1920 us; the launch traced here: 1910 us
  waiting for transfers between devices  982 us (51%)
  matrix products  491 us (26%)
  blocking collectives  172 us (9%)
  other arithmetic  125 us (7%)
  local copies, waits for them, and re-layouts  90 us (5%)
  starting transfers between devices  33.5 us (2%)
    psum x1, waiting for transfers between devices, per_device(): lax.psum(jnp.einsum('tpc,tdc->pd', grad_pair_low, cross_pair, preferred_e...  204 us
    psum x1, waiting for transfers between devices, per_device(): lax.psum(jnp.dot(self_mixed, self_output, preferred_element_type=jnp.floa...  128 us
    psum x1, waiting for transfers between devices, per_device(): lax.psum(summed[1].astype(jnp.bfloat16), 'rows').astype(jnp.float32)  116 us
    psum x1, waiting for transfers between devices, per_device(): lax.psum(jnp.dot(cross_mixed, cross_output, preferred_element_type=jnp.fl...  85.6 us
    all_gather x8, blocking collectives, owner_key_grads(): lax.all_gather(spread[:, :, 0].T, 'rows', axis=0, tiled=True)  75.1 us
    dot_general x16, matrix products, scaled_scores(): jnp.einsum('qhe,khe->hqk', queries, key_rows, preferred_element_type=jnp....  73.1 us
    all_gather x8, blocking collectives, owner_key_grads(): lax.all_gather(row_total[:, :, 0].T, 'rows', axis=0, tiled=True)  71.9 us
    psum x1, waiting for transfers between devices, per_device(): lax.psum(jnp.einsum('rf,df->rd', grad_pre, widen_weights, preferred_eleme...  68.7 us
  transfers between devices with their start and end apart: 46, of which 25 were waited for; matrix products, arithmetic and copies ran while one was open for 25% of the time, Pallas kernels for 0%

profile of v1, /device:TPU:0, one launch (start us, length us, event | category | flops | bytes accessed | tf_op | source)
XLA Modules:
  0.0 1912.8 jit_solution(11885370948672284006)
XLA Ops:
  36.8 9.3 all-gather.87.cloned.1.call-done
  54.1 17.5 all-gather.85.cloned.1.call-done
  78.5 19.1 all-gather.103.cloned.1.call-done
  105.2 17.8 all-gather.101.cloned.1.call-done
  128.6 20.3 %all-gather.95.cloned.1.call-done = bf16[1,2048,256]{1,2,0:T(8,128)(2,1)} async-done(((bf16[1,256,256]{1,2,0:T(8,128)(2,1)}), bf16[1,2048,256]{1,2,0:T(8,128)(2,1)}) %all-gather.95.cloned.1.call-update) | async-done | bytes 1048592 | tf_op jit(solution)/shard_map/all_gather | solution.py:172
  156.4 17.9 all-gather.93.cloned.1.call-done
  179.9 19.8 %all-gather.79.cloned.1.call-done = bf16[1,2048,256]{1,2,0:T(8,128)(2,1)} async-done(((bf16[1,256,256]{1,2,0:T(8,128)(2,1)}), bf16[1,2048,256]{1,2,0:T(8,128)(2,1)}) %all-gather.79.cloned.1.call-update) | async-done | bytes 1048592 | tf_op jit(solution)/shard_map/all_gather | solution.py:172
  210.0 15.2 all-gather.77.cloned.1.call-done
  265.8 9.5 all_gather.169
  275.3 9.1 all_gather.165
  284.4 8.0 all_gather.161
  292.4 9.1 all_gather.173
  333.6 128.3 %all-reduce.22.cloned.1.call-done = (f32[256,1024]{1,0:T(8,128)}, f32[256,1024]{1,0:T(8,128)}, f32[256,1024]{1,0:T(8,128)}, f32[256,1024]{1,0:T(8,128)}) async-done(((f32[256,1024]{1,0:T(8,128)}, f32[256,1024]{1,0:T(8,128)}, f32[256,1024]{1,0:T(8,128)}, f32[256,1024]{1,0:T(8,128)}), (f32[256,1024]{1,0:T(8,128)}, f32[256,1024]{1,0:T(8,128)}, f32[256,1024]{1,0:T(8,128)}, ...) | async-done | bytes 4194320 | tf_op jit(solution)/shard_map/psum | solution.py:178
  468.0 18.4 all-gather.115.cloned.1.call-done
  494.1 17.9 all-gather.107.cloned.1.call-done
  529.9 7.9 all-gather.91.cloned.1.call-done
  546.0 17.3 all-gather.89.cloned.1.call-done
  570.9 17.8 all-gather.83.cloned.1.call-done
  596.4 17.8 all-gather.81.cloned.1.call-done
  625.9 14.0 all-gather.105.cloned.1.call-done
  645.7 19.6 %all-gather.99.cloned.1.call-done = bf16[1,2048,256]{1,2,0:T(8,128)(2,1)} async-done(((bf16[1,256,256]{1,2,0:T(8,128)(2,1)}), bf16[1,2048,256]{1,2,0:T(8,128)(2,1)}) %all-gather.99.cloned.1.call-update) | async-done | bytes 1048592 | tf_op jit(solution)/shard_map/all_gather | solution.py:196
  674.4 16.5 all-gather.97.cloned.1.call-done
  698.6 10.0 all_gather.189
  708.6 9.1 all_gather.185
  717.7 9.0 all_gather.181
  726.7 8.1 all_gather.177
  739.5 6.2 exponential_divide_fusion
  761.4 6.9 all-gather.65.cloned.1.call-done
  768.3 6.2 exponential_divide_fusion.2
  774.5 19.4 %all-gather.61.cloned.1.call-done = bf16[2048,256]{0,1:T(8,128)(2,1)} async-done(((bf16[256,256]{0,1:T(8,128)(2,1)}), bf16[2048,256]{0,1:T(8,128)(2,1)}) %all-gather.61.cloned.1.call-update) | async-done | bytes 1048592 | tf_op jit(solution)/shard_map/all_gather | solution.py:93
  793.9 6.2 exponential_divide_fusion.3
  800.2 85.6 %all-reduce.32.cloned.1.call-done = (bf16[256,1024]{1,0:T(8,128)(2,1)}, bf16[256,1024]{1,0:T(8,128)(2,1)}, bf16[256,1024]{1,0:T(8,128)(2,1)}, bf16[256,1024]{1,0:T(8,128)(2,1)}) async-done(((bf16[256,1024]{1,0:T(8,128)(2,1)}, bf16[256,1024]{1,0:T(8,128)(2,1)}, bf16[256,1024]{1,0:T(8,128)(2,1)}, bf16[256,1024]{1,0:T(8,128)(2,1)}), (bf16[256,1024]{1,0:T(8,128)(2,1)}, bf16[256,1024]{1,0:T(8,128)(2,1)}, ...) | async-done | bytes 2097168 | tf_op jit(solution)/shard_map/psum | solution.py:203
  940.6 68.7 %all-reduce.30.cloned.1.call-done = (bf16[256,1024]{1,0:T(8,128)(2,1)}, bf16[256,1024]{1,0:T(8,128)(2,1)}, bf16[256,1024]{1,0:T(8,128)(2,1)}, bf16[256,1024]{1,0:T(8,128)(2,1)}) async-done(((bf16[256,1024]{1,0:T(8,128)(2,1)}, bf16[256,1024]{1,0:T(8,128)(2,1)}, bf16[256,1024]{1,0:T(8,128)(2,1)}, bf16[256,1024]{1,0:T(8,128)(2,1)}), (bf16[256,1024]{1,0:T(8,128)(2,1)}, bf16[256,1024]{1,0:T(8,128)(2,1)}, ...) | async-done | bytes 2097168 | tf_op jit(solution)/shard_map/psum | solution.py:234
  1019.0 7.0 multiply_reduce_fusion.5
  1026.5 7.7 multiply_reduce_fusion.3
  1035.3 7.3 multiply_reduce_fusion.1
  1042.5 9.0 all_gather.191
  1051.6 9.0 all_gather.187
  1060.6 7.5 fusion.173
  1069.7 7.0 multiply_reduce_fusion.7
  1076.7 8.5 all_gather.183
  1085.2 7.7 fusion.171
  1094.2 9.0 all_gather.179
  1103.2 7.5 fusion.177
  1112.0 7.9 fusion.175
  1156.7 6.9 fusion.167
  1179.6 61.5 %all-reduce.28.cloned.1.call-done = (bf16[256,1024]{1,0:T(8,128)(2,1)}, bf16[256,1024]{1,0:T(8,128)(2,1)}, bf16[256,1024]{1,0:T(8,128)(2,1)}, bf16[256,1024]{1,0:T(8,128)(2,1)}) async-done(((bf16[256,1024]{1,0:T(8,128)(2,1)}, bf16[256,1024]{1,0:T(8,128)(2,1)}, bf16[256,1024]{1,0:T(8,128)(2,1)}, bf16[256,1024]{1,0:T(8,128)(2,1)}), (bf16[256,1024]{1,0:T(8,128)(2,1)}, bf16[256,1024]{1,0:T(8,128)(2,1)}, ...) | async-done | bytes 2097168 | tf_op jit(solution)/shard_map/psum | solution.py:278
  1264.4 8.0 multiply_reduce_fusion.2
  1272.6 10.3 multiply_reduce_fusion.4
  1283.3 8.0 multiply_reduce_fusion.6
  1293.4 9.2 fusion.176
  1302.7 8.1 fusion.174
  1326.5 8.7 fusion.178
  1336.0 10.7 all_gather.171
  1346.7 9.3 all_gather.167
  1356.0 10.2 all_gather.163
  1366.2 9.3 all_gather.175
  1381.3 7.0 fusion.165
  1391.6 7.1 fusion.164
  1407.3 7.1 fusion.163
  1428.1 7.1 fusion.166
  1471.3 203.8 %all-reduce.26.cloned.1.call-done = (bf16[256,1024]{1,0:T(8,128)(2,1)}, bf16[256,1024]{1,0:T(8,128)(2,1)}, bf16[256,1024]{1,0:T(8,128)(2,1)}, bf16[256,1024]{1,0...) async-done(((bf16[256,1024]{1,0:T(8,128)(2,1)}, ...) | async-done | bytes 6291472 | tf_op jit(solution)/shard_map/psum | solution.py:284
  1722.4 24.8 %all-reduce.9 = (bf16[32,2,256]{2,1,0:T(2,128)(2,1)S(1)}, bf16[256]{0:T(256)(128)(2,1)S(1)}, bf16[256]{0:T(256)(128)(2,1)S(1)}) all-reduce(bf16[32,2,256]{2,1,0:T(2,128)(2,1)S(1)} %dynamic-slice_convert_fusion, bf16[256]{0:T(256)(128)(2,1)S(1)} %dynamic_slice.40, ...), channel_id=1, replica_groups=mesh['heads'=4,'rows'=8] {'rows'}, use_global_device_ids=true, to_apply=%region_100.101 | all-reduce | flops 16896 | bytes 67584 | tf_op jit(solution)/shard_map/psum | solution.py:364
  1769.3 116.2 %all-reduce.24.cloned.1.call-done = (bf16[3,1024,256]{1,2,0:T(8,128)(2,1)}, bf16[2,1024,256]{1,2,0:T(8,128)(2,1)}, bf16[768,256]{0,1:T(8,128)(2,1)}, bf16[256,10...) async-done(((bf16[3,1024,256]{1,2,0:T(8,128)(2,1)}, ...) | async-done | bytes 8781840 | tf_op jit(solution)/shard_map/psum | solution.py:365
  (1076 shorter events, 581.7 us)
Async XLA Ops:
  7.2 881.4 %copy-start = (bf16[1024,1024]{1,0:T(8,128)(2,1)S(1)}, bf16[1024,1024]{1,0:T(8,128)(2,1)}, u32[]{:S(2)}) copy-start(bf16[1024,1024]{1,0:T(8,128)(2,1)} %param.29) | copy-start | bytes 6291460
  7.2 38.9 %all-gather.87.cloned.1.call-start = ((), (), s32[]{:S(2)}) async-start(), calls=%async_computation.25 | async-start | bytes 1179648 | tf_op jit(solution)/shard_map/all_gather | solution.py:172
  19.6 51.9 %all-gather.85.cloned.1.call-start = ((), (), s32[]{:S(2)}) async-start(), calls=%async_computation.24 | async-start | bytes 1179648 | tf_op jit(solution)/shard_map/all_gather | solution.py:173
  20.4 77.2 %all-gather.103.cloned.1.call-start = ((), (), s32[]{:S(2)}) async-start(), calls=%async_computation.33 | async-start | bytes 1179648 | tf_op jit(solution)/shard_map/all_gather | solution.py:172
  23.4 99.6 %all-gather.101.cloned.1.call-start = ((), (), s32[]{:S(2)}) async-start(), calls=%async_computation.32 | async-start | bytes 1179648 | tf_op jit(solution)/shard_map/all_gather | solution.py:173
  24.0 124.9 %all-gather.95.cloned.1.call-start = ((), (), s32[]{:S(2)}) async-start(), calls=%async_computation.29 | async-start | bytes 1179648 | tf_op jit(solution)/shard_map/all_gather | solution.py:172
  26.9 147.3 %all-gather.93.cloned.1.call-start = ((), (), s32[]{:S(2)}) async-start(), calls=%async_computation.28 | async-start | bytes 1179648 | tf_op jit(solution)/shard_map/all_gather | solution.py:173
  27.5 172.2 %all-gather.79.cloned.1.call-start = ((), (), s32[]{:S(2)}) async-start(), calls=%async_computation.21 | async-start | bytes 1179648 | tf_op jit(solution)/shard_map/all_gather | solution.py:172
  33.9 191.3 %all-gather.77.cloned.1.call-start = ((), (), s32[]{:S(2)}) async-start(), calls=%async_computation.20 | async-start | bytes 1179648 | tf_op jit(solution)/shard_map/all_gather | solution.py:173
  34.7 270.8 %all-gather.113.cloned.1.call-start = ((), (), s32[]{:S(2)}) async-start(), calls=%async_computation.38 | async-start | bytes 1179648 | tf_op jit(solution)/shard_map/all_gather | solution.py:93
  35.4 281.1 %all-gather.111.cloned.1.call-start = ((), (), s32[]{:S(2)}) async-start(), calls=%async_computation.37 | async-start | bytes 1179648 | tf_op jit(solution)/shard_map/all_gather | solution.py:93
  36.0 291.6 %all-gather.109.cloned.1.call-start = ((), (), s32[]{:S(2)}) async-start(), calls=%async_computation.36 | async-start | bytes 1179648 | tf_op jit(solution)/shard_map/all_gather | solution.py:93
  36.7 425.2 %all-reduce.22.cloned.1.call-start = ((), (), s32[]{:S(2)}) async-start(), calls=%async_computation.40 | async-start | bytes 8388608 | tf_op jit(solution)/shard_map/psum | solution.py:178
  54.1 221.2 %copy-start.256 = (f32[4,256]{1,0:T(4,128)}, f32[4,256]{1,0:T(4,128)S(1)}, u32[]{:S(2)}) copy-start(f32[4,256]{1,0:T(4,128)S(1)} %fusion.7) | copy-start | bytes 12292
  100.2 222.5 %copy-start.223 = (f32[4,256]{1,0:T(4,128)}, f32[4,256]{1,0:T(4,128)S(1)}, u32[]{:S(2)}) copy-start(f32[4,256]{1,0:T(4,128)S(1)} %get-tuple-element.229) | copy-start | bytes 12292
  232.8 253.7 %all-gather.115.cloned.1.call-start = ((), (), s32[]{:S(2)}) async-start(), calls=%async_computation.39 | async-start | bytes 1179648 | tf_op jit(solution)/shard_map/all_gather | solution.py:93
  233.6 278.4 %all-gather.107.cloned.1.call-start = ((), (), s32[]{:S(2)}) async-start(), calls=%async_computation.35 | async-start | bytes 1179648 | tf_op jit(solution)/shard_map/all_gather | solution.py:196
  237.9 299.8 %all-gather.91.cloned.1.call-start = ((), (), s32[]{:S(2)}) async-start(), calls=%async_computation.27 | async-start | bytes 1179648 | tf_op jit(solution)/shard_map/all_gather | solution.py:196
  242.2 321.0 %all-gather.89.cloned.1.call-start = ((), (), s32[]{:S(2)}) async-start(), calls=%async_computation.26 | async-start | bytes 1179648 | tf_op jit(solution)/shard_map/all_gather | solution.py:197
  242.8 345.9 %all-gather.83.cloned.1.call-start = ((), (), s32[]{:S(2)}) async-start(), calls=%async_computation.23 | async-start | bytes 1179648 | tf_op jit(solution)/shard_map/all_gather | solution.py:196
  247.0 367.2 %all-gather.81.cloned.1.call-start = ((), (), s32[]{:S(2)}) async-start(), calls=%async_computation.22 | async-start | bytes 1179648 | tf_op jit(solution)/shard_map/all_gather | solution.py:197
  247.6 392.2 %all-gather.105.cloned.1.call-start = ((), (), s32[]{:S(2)}) async-start(), calls=%async_computation.34 | async-start | bytes 1179648 | tf_op jit(solution)/shard_map/all_gather | solution.py:197
  248.4 417.0 %all-gather.99.cloned.1.call-start = ((), (), s32[]{:S(2)}) async-start(), calls=%async_computation.31 | async-start | bytes 1179648 | tf_op jit(solution)/shard_map/all_gather | solution.py:196
  252.1 438.8 %all-gather.97.cloned.1.call-start = ((), (), s32[]{:S(2)}) async-start(), calls=%async_computation.30 | async-start | bytes 1179648 | tf_op jit(solution)/shard_map/all_gather | solution.py:197
  258.1 760.8 %copy-start.214 = (f32[2048]{0:T(1024)}, f32[2048]{0:T(1024)S(1)}, u32[]{:S(2)}) copy-start(f32[2048]{0:T(1024)S(1)} %fusion.404) | copy-start | bytes 24580
  260.0 354.2 %copy-start.212 = (f32[2048]{0:T(1024)}, f32[2048]{0:T(1024)S(1)}, u32[]{:S(2)}) copy-start(f32[2048]{0:T(1024)S(1)} %fusion.403) | copy-start | bytes 24580
  261.2 266.7 %copy-start.154 = (f32[1024]{0:T(1024)}, f32[1024]{0:T(1024)S(1)}, u32[]{:S(2)}) copy-start(f32[1024]{0:T(1024)S(1)} %convert_element_type.678) | copy-start | bytes 12292
  262.5 39.1 %all-to-all-start.2 = ((f32[8,256,4]{1,2,0:T(4,128)}), f32[8,256,4]{1,2,0:T(4,128)S(1)}, u32[]{:S(2)}, u32[]{:S(2)}) async-start(f32[8,256,4]{1,2,0:T(4,128)} %stack.81), calls=%async_computation.2 | async-start | bytes 65536 | tf_op jit(solution)/shard_map/all_to_all | solution.py:98
  302.2 9.4 all-to-all-start.1
  312.2 10.5 all-to-all-start
  323.4 163.1 %all-to-all-start.3 = ((f32[8,256,4]{1,2,0:T(4,128)}), f32[8,256,4]{1,2,0:T(4,128)S(1)}, u32[]{:S(2)}, u32[]{:S(2)}) async-start(f32[8,256,4]{1,2,0:T(4,128)} %stack.84), calls=%async_computation.3 | async-start | bytes 65536 | tf_op jit(solution)/shard_map/all_to_all | solution.py:98
  327.6 411.9 %all-gather.73.cloned.1.call-start = ((), (), s32[]{:S(2)}) async-start(), calls=%async_computation.18 | async-start | bytes 1179648 | tf_op jit(solution)/shard_map/all_gather | solution.py:93
  466.5 431.9 %copy-start.7 = (f32[256,1024]{1,0:T(8,128)}, f32[256,1024]{1,0:T(8,128)S(1)}, u32[]{:S(2)}) copy-start(f32[256,1024]{1,0:T(8,128)S(1)} %get-tuple-element.181) | copy-start | bytes 3145732
  468.0 282.4 %all-gather.69.cloned.1.call-start = ((), (), s32[]{:S(2)}) async-start(), calls=%async_computation.16 | async-start | bytes 1179648 | tf_op jit(solution)/shard_map/all_gather | solution.py:93
  518.4 216.5 %all-to-all-start.7 = ((f32[8,256,4]{1,2,0:T(4,128)}), f32[8,256,4]{1,2,0:T(4,128)}, u32[]{:S(2)}, u32[]{:S(2)}) async-start(f32[8,256,4]{1,2,0:T(4,128)} %stack.192), calls=%async_computation.7 | async-start | bytes 65536 | tf_op jit(solution)/shard_map/all_to_all | solution.py:98
  522.3 246.0 %all-gather.65.cloned.1.call-start = ((), (), s32[]{:S(2)}) async-start(), calls=%async_computation.14 | async-start | bytes 1179648 | tf_op jit(solution)/shard_map/all_gather | solution.py:93
  529.8 264.1 %all-gather.61.cloned.1.call-start = ((), (), s32[]{:S(2)}) async-start(), calls=%async_computation.12 | async-start | bytes 1179648 | tf_op jit(solution)/shard_map/all_gather | solution.py:93
  540.4 478.5 %copy-start.237 = (f32[4,256]{1,0:T(4,128)}, f32[4,256]{1,0:T(4,128)S(1)}, u32[]{:S(2)}) copy-start(f32[4,256]{1,0:T(4,128)S(1)} %get-tuple-element.241) | copy-start | bytes 12292
  546.0 473.0 %copy-start.267 = (f32[4,256]{1,0:T(4,128)}, f32[4,256]{1,0:T(4,128)S(1)}, u32[]{:S(2)}) copy-start(f32[4,256]{1,0:T(4,128)S(1)} %fusion.15) | copy-start | bytes 12292
  625.8 260.0 %all-reduce.32.cloned.1.call-start = ((), (), s32[]{:S(2)}) async-start(), calls=%async_computation.45 | async-start | bytes 4194304 | tf_op jit(solution)/shard_map/psum | solution.py:203
  735.4 10.2 all-to-all-start.6
  746.3 10.3 all-to-all-start.5
  757.2 17.3 all-to-all-start.4
  761.3 248.0 %all-reduce.30.cloned.1.call-start = ((), (), s32[]{:S(2)}) async-start(), calls=%async_computation.44 | async-start | bytes 4194304 | tf_op jit(solution)/shard_map/psum | solution.py:234
  922.2 200.2 %all-gather.75.cloned.1.call-start = ((), (), s32[]{:S(2)}) async-start(), calls=%async_computation.19 | async-start | bytes 1179648 | tf_op jit(solution)/shard_map/all_gather | solution.py:94
  1035.2 98.1 %all-gather.71.cloned.1.call-start = ((), (), s32[]{:S(2)}) async-start(), calls=%async_computation.17 | async-start | bytes 1179648 | tf_op jit(solution)/shard_map/all_gather | solution.py:94
  1076.6 68.1 %all-gather.67.cloned.1.call-start = ((), (), s32[]{:S(2)}) async-start(), calls=%async_computation.15 | async-start | bytes 1179648 | tf_op jit(solution)/shard_map/all_gather | solution.py:94
  1094.1 62.6 %all-gather.63.cloned.1.call-start = ((), (), s32[]{:S(2)}) async-start(), calls=%async_computation.13 | async-start | bytes 1179648 | tf_op jit(solution)/shard_map/all_gather | solution.py:94
  1111.9 129.2 %all-reduce.28.cloned.1.call-start = ((), (), s32[]{:S(2)}) async-start(), calls=%async_computation.43 | async-start | bytes 4194304 | tf_op jit(solution)/shard_map/psum | solution.py:278
  1122.3 253.7 %all-gather.57.cloned.1.call-start = ((), (), s32[]{:S(2)}) async-start(), calls=%async_computation.10 | async-start | bytes 1179648 | tf_op jit(solution)/shard_map/all_gather | solution.py:94
  1258.5 133.1 %all-gather.55.cloned.1.call-start = ((), (), s32[]{:S(2)}) async-start(), calls=%async_computation.9 | async-start | bytes 1179648 | tf_op jit(solution)/shard_map/all_gather | solution.py:94
  1272.5 134.8 %all-gather.53.cloned.1.call-start = ((), (), s32[]{:S(2)}) async-start(), calls=%async_computation.8 | async-start | bytes 1179648 | tf_op jit(solution)/shard_map/all_gather | solution.py:94
  1291.3 131.6 %all-gather.59.cloned.1.call-start = ((), (), s32[]{:S(2)}) async-start(), calls=%async_computation.11 | async-start | bytes 1179648 | tf_op jit(solution)/shard_map/all_gather | solution.py:94
  1375.6 299.5 %all-reduce.26.cloned.1.call-start = ((), (), s32[]{:S(2)}) async-start(), calls=%async_computation.42 | async-start | bytes 12582912 | tf_op jit(solution)/shard_map/psum | solution.py:284
  1449.4 436.1 %all-reduce.24.cloned.1.call-start = ((), (), s32[]{:S(2)}) async-start(), calls=%async_computation.41 | async-start | bytes 17563648 | tf_op jit(solution)/shard_map/psum | solution.py:365
  1469.3 211.9 %copy-start.4 = (bf16[4,256,1024]{2,1,0:T(8,128)(2,1)S(1)}, bf16[4,256,1024]{2,1,0:T(8,128)(2,1)}, u32[]{:S(2)}) copy-start(bf16[4,256,1024]{2,1,0:T(8,128)(2,1)} %param.16) | copy-start | bytes 6291460
  1469.4 211.9 %copy-start.240 = (f32[256]{0:T(256)S(1)}, f32[256]{0:T(256)}, u32[]{:S(2)}) copy-start(f32[256]{0:T(256)} %copy-done.239) | copy-start | bytes 3076
  1469.4 211.9 %copy-start.242 = (f32[256]{0:T(256)S(1)}, f32[256]{0:T(256)}, u32[]{:S(2)}) copy-start(f32[256]{0:T(256)} %copy-done.241) | copy-start | bytes 3076
  1469.4 211.9 %copy-start.244 = (f32[256]{0:T(256)S(1)}, f32[256]{0:T(256)}, u32[]{:S(2)}) copy-start(f32[256]{0:T(256)} %copy-done.243) | copy-start | bytes 3076
  1469.4 211.9 %copy-start.246 = (f32[256]{0:T(256)S(1)}, f32[256]{0:T(256)}, u32[]{:S(2)}) copy-start(f32[256]{0:T(256)} %copy-done.245) | copy-start | bytes 3076
  1471.3 217.2 %copy-start.297 = (f32[256]{0:T(256)S(1)}, f32[256]{0:T(256)}, u32[]{:S(2)}) copy-start(f32[256]{0:T(256)} %copy-done.296) | copy-start | bytes 3076
  1471.3 217.2 %copy-start.295 = (f32[256]{0:T(256)S(1)}, f32[256]{0:T(256)}, u32[]{:S(2)}) copy-start(f32[256]{0:T(256)} %copy-done.294) | copy-start | bytes 3076
  1471.3 217.3 %copy-start.277 = (f32[256]{0:T(256)S(1)}, f32[256]{0:T(256)}, u32[]{:S(2)}) copy-start(f32[256]{0:T(256)} %copy-done.276) | copy-start | bytes 3076
  1471.3 217.3 %copy-start.279 = (f32[256]{0:T(256)S(1)}, f32[256]{0:T(256)}, u32[]{:S(2)}) copy-start(f32[256]{0:T(256)} %copy-done.278) | copy-start | bytes 3076
  (312 other events, 5575.6 us)
Sparse Core Ops, SparseCore 0:
  19.8 26.2 all-gather.86
  47.9 23.5 all-gather.84
  74.0 23.5 all-gather.102
  99.4 23.5 all-gather.100
  125.3 23.5 all-gather.94
  150.6 23.5 all-gather.92
  176.1 23.5 all-gather.78
  201.6 23.5 all-gather.76
  227.7 23.5 all-gather.112
  253.0 23.6 all-gather.110
  278.5 23.6 all-gather.108
  305.9 156.0 all-reduce.21
  463.9 22.5 all-gather.114
  488.4 23.5 all-gather.106
  513.9 23.8 all-gather.90
  539.6 23.5 all-gather.88
  565.1 23.5 all-gather.82
  590.6 23.5 all-gather.80
  616.2 23.5 all-gather.104
  641.7 23.5 all-gather.98
  667.4 23.5 all-gather.96
  693.0 23.7 all-gather.72
  718.8 23.6 all-gather.68
  744.3 23.9 all-gather.64
  770.3 23.5 all-gather.60
  797.7 88.0 all-reduce.31
  922.3 86.9 all-reduce.29
  1035.3 22.6 all-gather.74
  1076.8 21.6 all-gather.70
  1100.3 23.6 all-gather.66
  1126.6 23.6 all-gather.62
  1153.0 88.0 all-reduce.27
  1258.6 22.4 all-gather.56
  1283.1 23.5 all-gather.54
  1309.1 23.6 all-gather.52
  1375.7 21.9 all-gather.58
  1449.5 225.5 all-reduce.25
  1755.1 130.3 all-reduce.23
